TPU v7x, 32 devices: a whole 2x2x4 slice. The times are simulated.
32 devices in a mesh: groups: 2 (over y), seq: 16 (over z, x, core).
Axes of the slice: x: 2, y: 2, z: 4, core: 2. Of those that a mesh axis runs over, the one named last changes fastest.
Arguments:
- queries: bfloat16 [4096, 1536], P(('groups', 'seq')), parts along dimension 0, may hold values from -6 to 6
- keys: bfloat16 [4096, 1536], P(('groups', 'seq')), parts along dimension 0, may hold values from -6 to 6
- values: bfloat16 [4096, 1536], P(('groups', 'seq')), parts along dimension 0, may hold values from -6 to 6
- w_out: bfloat16 [1536, 3072], replicated, may hold values from -0.15625 to 0.15625
- shift_mod: float32 [6144], P('groups'), parts along dimension 0, may hold values from -5 to 5
- scale_mod: float32 [6144], P('groups'), parts along dimension 0, may hold values from -3 to 3
- w_final: bfloat16 [3072, 64], replicated, may hold values from -0.109375 to 0.109375
- conv_weight: bfloat16 [432, 512], replicated, may hold values from -0.3125 to 0.3125
- conv_bias: float32 [512], replicated, may hold values from -3 to 3
Outputs:
- decoded: bfloat16 [8, 32, 64, 512], P('groups', 'seq'), parts along dimension 0
There are 2 independent parts, one for each index of `groups`. A program takes and returns all parts, laid end to end along the dimension named above; an argument that names none is the same for every part. Nothing has to cross between parts.
All inputs are finite; a program needn't handle non-finite values.
Results may differ from a plain program's by a relative error of at most 0.018.
Values may be sent and summed in bfloat16 or wider, within the bound.
A program may use at most 192 MiB of HBM per device.

v0:
```python
import math
import jax
import jax.numpy as jnp
from jax import lax
from jax.sharding import PartitionSpec as P

HEADS = 12
HEAD_DIM = 128
HEAD_GROUPS = 4
LATENT_CH = 16
FRAMES = 4
ROWS = 32
COLS_DEV = 1


def with_halo(cells, sides, width):
    for axis, dim in sides:
        count = lax.axis_size(axis)
        ends = count - 1
        head = lax.slice_in_dim(cells, 0, width, axis=dim)
        tail = lax.slice_in_dim(cells, cells.shape[dim] - width, cells.shape[dim], axis=dim)
        cells = jnp.concatenate(
            [
                lax.ppermute(tail, axis, [(i, (i + 1) % count) for i in range(ends)]),
                cells,
                lax.ppermute(head, axis, [((i + 1) % count, i) for i in range(ends)]),
            ],
            axis=dim,
        )
    return cells


def to_pieces(source, blocks):
    piece_rows = source.shape[0] // blocks
    grouped = source.reshape(blocks, piece_rows, HEAD_GROUPS, source.shape[1] // HEAD_GROUPS)
    return jnp.transpose(grouped, (0, 2, 1, 3)).reshape(
        blocks * HEAD_GROUPS, piece_rows, source.shape[1] // HEAD_GROUPS
    )


def absorb(state, key_part, value_part, query_rows):
    key_count = key_part.shape[0]
    block_rows = min(key_count, max(128, 1048576 // query_rows.shape[0]))
    per_head = HEADS // HEAD_GROUPS
    key_blocks = key_part.reshape(key_count // block_rows, block_rows, per_head, HEAD_DIM)
    value_blocks = value_part.reshape(key_count // block_rows, block_rows, per_head, HEAD_DIM)
    inv_root = 1.0 / math.sqrt(HEAD_DIM)

    def one_block(state_in, kv_block):
        run_max, run_sum, accumulated = state_in
        key_block, value_block = kv_block
        scores = (
            jnp.einsum("qhd,khd->hqk", query_rows, key_block, preferred_element_type=jnp.float32)
            * inv_root
        )
        new_max = jnp.maximum(run_max, jnp.max(scores, axis=2))
        factor = jnp.exp(run_max - new_max)
        exp_scores = jnp.exp(scores - new_max[:, :, None])
        run_sum = run_sum * factor + jnp.sum(exp_scores, axis=2)
        update = jnp.einsum(
            "hqk,khd->hqd",
            exp_scores.astype(jnp.bfloat16),
            value_block,
            preferred_element_type=jnp.float32,
        )
        accumulated = accumulated * factor[:, :, None] + update
        return ((new_max, run_sum, accumulated), None)

    state, unused = lax.scan(one_block, state, (key_blocks, value_blocks))
    return state


def fresh_state(per_head, count):
    return (
        jnp.full((per_head, count), -1e30, jnp.float32),
        jnp.zeros((per_head, count), jnp.float32),
        jnp.zeros((per_head, count, HEAD_DIM), jnp.float32),
    )


def convolve(padded, conv_weight, conv_bias, frames, width, height):
    taps = []
    for shift_t in range(3):
        for shift_x in range(3):
            for shift_y in range(3):
                taps.append(
                    padded[
                        shift_t : shift_t + frames,
                        shift_x : shift_x + width,
                        shift_y : shift_y + height,
                        :,
                    ]
                )
    stacked = jnp.concatenate(taps, axis=3)
    flat = stacked.reshape(frames * width * height, stacked.shape[3])
    output = jnp.dot(flat, conv_weight, preferred_element_type=jnp.float32) + conv_bias
    return output.astype(jnp.bfloat16).reshape(frames, width, height, conv_weight.shape[1])


def shards(queries, keys, values, w_out, shift_mod, scale_mod, w_final, conv_weight, conv_bias):
    devices = lax.axis_size("seq")
    position = lax.axis_index("seq")
    tok_dev = queries.shape[0]
    blocks = devices // HEAD_GROUPS
    per_head = HEADS // HEAD_GROUPS
    group_width = per_head * HEAD_DIM
    query_count = tok_dev * HEAD_GROUPS
    got_queries = lax.all_to_all(
        to_pieces(queries, blocks), "seq", split_axis=0, concat_axis=1, tiled=True
    )
    query_rows = got_queries.reshape(query_count, per_head, HEAD_DIM)
    key_groups = jnp.transpose(keys.reshape(tok_dev, HEAD_GROUPS, group_width), (1, 0, 2))
    value_groups = jnp.transpose(values.reshape(tok_dev, HEAD_GROUPS, group_width), (1, 0, 2))
    key_copies = jnp.broadcast_to(
        key_groups[None], (blocks, HEAD_GROUPS, tok_dev, group_width)
    ).reshape(devices, tok_dev, group_width)
    value_copies = jnp.broadcast_to(
        value_groups[None], (blocks, HEAD_GROUPS, tok_dev, group_width)
    ).reshape(devices, tok_dev, group_width)
    all_keys, all_values = (
        lax.all_to_all(key_copies, "seq", split_axis=0, concat_axis=1, tiled=True),
        lax.all_to_all(value_copies, "seq", split_axis=0, concat_axis=1, tiled=True),
    )
    state = absorb(fresh_state(per_head, query_count), all_keys[0], all_values[0], query_rows)
    run_max, run_sum, accumulated = state
    result = (accumulated / run_sum[:, :, None]).astype(jnp.bfloat16)
    result = jnp.transpose(result, (1, 0, 2)).reshape(1, query_count, group_width)
    returned = lax.all_to_all(result, "seq", split_axis=1, concat_axis=0, tiled=True)
    piece_rows = tok_dev // blocks
    attended = jnp.transpose(
        returned.reshape(blocks, HEAD_GROUPS, piece_rows, group_width), (0, 2, 1, 3)
    ).reshape(tok_dev, HEADS * HEAD_DIM)
    projected = jnp.dot(attended, w_out, preferred_element_type=jnp.float32)
    centered = projected - jnp.mean(projected, axis=1, keepdims=True)
    variance = jnp.mean(centered * centered, axis=1, keepdims=True)
    normed = (centered * lax.rsqrt(variance + 1e-06) * (1.0 + scale_mod) + shift_mod).astype(
        jnp.bfloat16
    )
    patches = jnp.dot(normed, w_final, preferred_element_type=jnp.float32).astype(jnp.bfloat16)
    rows_dev = FRAMES * ROWS // devices
    columns = COLS_DEV * devices
    laid = patches.reshape(rows_dev, columns, 4 * LATENT_CH)
    tile = lax.all_to_all(laid, "seq", split_axis=1, concat_axis=0, tiled=True)
    latent = tile.reshape(FRAMES, ROWS, COLS_DEV, LATENT_CH, 2, 2).transpose(0, 2, 5, 1, 4, 3)
    latent = latent.reshape(FRAMES, 2 * COLS_DEV, 2 * ROWS, LATENT_CH)
    rimmed = with_halo(latent, (("seq", 1),), 1)
    left_rim = jnp.where(position == 0, latent[:, :1], rimmed[:, :1])
    right_rim = jnp.where(position == devices - 1, latent[:, -1:], rimmed[:, -1:])
    widened = jnp.concatenate([left_rim, latent, right_rim], axis=1)
    padded = jnp.pad(widened, ((2, 0), (0, 0), (1, 1), (0, 0)), mode="edge")
    return convolve(padded, conv_weight, conv_bias, FRAMES, 2 * COLS_DEV, 2 * ROWS)


def solution(mesh):
    placed = (
        P(("groups", "seq"), None),
        P(("groups", "seq"), None),
        P(("groups", "seq"), None),
        P(),
        P("groups"),
        P("groups"),
        P(),
        P(),
        P(),
    )
    return jax.shard_map(
        shards,
        mesh=mesh,
        in_specs=placed,
        out_specs=P("groups", "seq", None, None),
        check_vma=False,
    )
```

profile of v0, /device:TPU:3, one launch (start us, length us, event | category | flops | bytes accessed | tf_op | source)
XLA Modules:
  0.0 180.4 jit_solution(2948887893393950316)
XLA Ops:
  0.0 1.2 reshape.125
  1.2 0.8 copy.31
  2.0 6.6 %all-to-all-start = ((bf16[16,32,384]{2,1,0:T(8,128)(2,1)}), bf16[16,32,384]{2,1,0:T(8,128)(2,1)S(1)}, u32[]{:S(2)}, u32[]{:S(2)}) async-start(bf16[16,32,384]{2,1,0:T(8,128)(2,1)} %bitcast.1), calls=%async_computation | async-start | bytes 786432 | tf_op jit(solution)/shard_map/all_to_all | solution.py:108
  8.7 0.3 copy.32
  9.0 10.7 %all-to-all-done = bf16[16,32,384]{2,1,0:T(8,128)(2,1)S(1)} async-done(((bf16[16,32,384]{2,1,0:T(8,128)(2,1)}), bf16[16,32,384]{2,1,0:T(8,128)(2,1)S(1)}, u32[]{:S(2)}, u32[]{:S(2)}) %all-to-all-start) | async-done | bytes 393248 | tf_op jit(solution)/shard_map/all_to_all | solution.py:108
  19.7 1.5 broadcast_in_dim.15
  21.2 4.8 %all-to-all-start.1 = ((bf16[16,128,384]{1,2,0:T(8,128)(2,1)}), bf16[16,128,384]{1,2,0:T(8,128)(2,1)S(1)}, u32[]{:S(2)}, u32[]{:S(2)}) async-start(bf16[16,128,384]{1,2,0:T(8,128)(2,1)} %bitcast.87), calls=%async_computation.1 | async-start | bytes 3145728 | tf_op jit(solution)/shard_map/all_to_all | solution.py:121
  26.1 0.3 copy.36
  26.4 33.1 %all-to-all-done.1 = bf16[16,128,384]{1,2,0:T(8,128)(2,1)S(1)} async-done(((bf16[16,128,384]{1,2,0:T(8,128)(2,1)}), bf16[16,128,384]{1,2,0:T(8,128)(2,1)S(1)}, u32[]{:S(2)}, u32[]{:S(2)}) %all-to-all-start.1) | async-done | bytes 1572896 | tf_op jit(solution)/shard_map/all_to_all | solution.py:121
  59.5 1.7 broadcast_in_dim.16
  61.2 7.5 %all-to-all-start.2 = ((bf16[16,128,384]{1,2,0:T(8,128)(2,1)}), bf16[16,128,384]{1,2,0:T(8,128)(2,1)S(1)}, u32[]{:S(2)}, u32[]{:S(2)}) async-start(bf16[16,128,384]{1,2,0:T(8,128)(2,1)} %bitcast.86), calls=%async_computation.2 | async-start | bytes 3145728 | tf_op jit(solution)/shard_map/all_to_all | solution.py:122
  68.8 3.6 %copy.33 = bf16[16,128,384]{1,0,2:T(8,128)(2,1)} copy(bf16[16,128,384]{1,2,0:T(8,128)(2,1)} %copy-done.2) | data formatting | bytes 3145728 | tf_op jit(solution)/shard_map/all_to_all | solution.py:121
  72.4 3.7 %squeeze.9 = bf16[2048,3,128]{0,2,1:T(8,128)(2,1)} reshape(bf16[16,128,384]{1,0,2:T(8,128)(2,1)} %copy.33) | data formatting | bytes 3145728 | tf_op jit(solution)/shard_map/while/body/jit(dynamic_index_in_dim)/squeeze | solution.py:69
  76.1 3.3 %multiply_reduce_fusion = (f32[3,512]{1,0:T(4,128)S(1)}, f32[3,512,2048]{2,1,0:T(8,128)S(1)}) fusion(bf16[2048,3,128]{0,2,1:T(8,128)(2,1)} %squeeze.9, bf16[512,3,128]{2,1,0:T(4,128)(2,1)S(1)} %reshape.127), kind=kOutput, calls=%fused_computation.1 | convolution fusion | flops 811596288 | bytes 14555136 | tf_op jit(solution)/shard_map/while/body/eval_jaxpr/qhd,khd->hqk/dot_general | solution.py:53
  79.4 2.5 %fusion = f32[3,512]{1,0:T(4,128)S(1)} fusion(f32[3,512,2048]{2,1,0:T(8,128)S(1)} %get-tuple-element.63, f32[3,512]{1,0:T(4,128)S(1)} %get-tuple-element.61), kind=kLoop, calls=%fused_computation.2 | loop fusion | flops 9435648 | bytes 12595200 | tf_op jit(solution)/shard_map/while/body/eval_jaxpr/reduce_sum | solution.py:59
  81.9 2.0 %copy-done.1 = f32[3,512,2048]{2,1,0:T(8,128)} copy-done((f32[3,512,2048]{2,1,0:T(8,128)}, f32[3,512,2048]{2,1,0:T(8,128)S(1)}, u32[]{:S(2)}) %copy-start.1) | copy-done | bytes 12582936
  83.9 18.2 %all-to-all-done.2 = bf16[16,128,384]{1,2,0:T(8,128)(2,1)S(1)} async-done(((bf16[16,128,384]{1,2,0:T(8,128)(2,1)}), bf16[16,128,384]{1,2,0:T(8,128)(2,1)S(1)}, u32[]{:S(2)}, u32[]{:S(2)}) %all-to-all-start.2) | async-done | bytes 1572896 | tf_op jit(solution)/shard_map/all_to_all | solution.py:122
  102.2 2.2 %copy.37 = bf16[16,128,384]{1,0,2:T(8,128)(2,1)} copy(bf16[16,128,384]{1,2,0:T(8,128)(2,1)S(1)} %all-to-all-done.2) | data formatting | bytes 3145728 | tf_op jit(solution)/shard_map/all_to_all | solution.py:122
  104.3 2.5 %squeeze.10 = bf16[2048,3,128]{0,2,1:T(8,128)(2,1)S(1)} reshape(bf16[16,128,384]{1,0,2:T(8,128)(2,1)} %copy.37) | data formatting | bytes 3145728 | tf_op jit(solution)/shard_map/while/body/jit(dynamic_index_in_dim)/squeeze | solution.py:69
  106.9 7.1 %fusion.16 = bf16[512,3,128]{0,2,1:T(8,128)(2,1)S(1)} fusion(bf16[2048,3,128]{0,2,1:T(8,128)(2,1)S(1)} %squeeze.10, f32[3,512,2048]{2,1,0:T(8,128)} %copy-done.1, f32[3,512]{1,0:T(4,128)S(1)} %get-tuple-element.61, f32[512,3]{0,1:T(4,128)S(1)} %bitcast_add_fusion, f32[512,3]{0,1:T(4,128)S(1)} %get-tuple-element.60), kind=kOutput, calls=%fused_computation.15 | convolution fusion | flops 815333376 | bytes 14567424 | tf_op jit(solution)/shard_map/while/body/eval_jaxpr/hqk,khd->hqd/dot_general | solution.py:60
  114.0 1.1 copy.38
  115.2 0.5 broadcast.84
  115.7 3.0 %reduce = bf16[512,384]{1,0:T(8,128)(2,1)S(1)} reduce(bf16[512,1,384]{2,1,0:T(2,128)(2,1)S(1)} %bitcast.92, bf16[]{:T(256)} %broadcast.84), dimensions={1}, to_apply=%bitcast.71.reduce_sub_computation | reduce | bytes 786434
  118.7 0.8 reshape.140
  119.5 7.5 %all-to-all-start.3 = ((bf16[16,2,6144]{2,1,0:T(2,128)(2,1)}), bf16[16,2,6144]{2,1,0:T(2,128)(2,1)S(1)}, u32[]{:S(2)}, u32[]{:S(2)}) async-start(bf16[16,2,6144]{2,1,0:T(2,128)(2,1)} %reshape.140), calls=%async_computation.3 | async-start | bytes 786432 | tf_op jit(solution)/shard_map/all_to_all | solution.py:128
  127.1 11.1 %all-to-all-done.3 = bf16[16,2,6144]{2,1,0:T(2,128)(2,1)S(1)} async-done(((bf16[16,2,6144]{2,1,0:T(2,128)(2,1)}), bf16[16,2,6144]{2,1,0:T(2,128)(2,1)S(1)}, u32[]{:S(2)}, u32[]{:S(2)}) %all-to-all-start.3) | async-done | bytes 393248 | tf_op jit(solution)/shard_map/all_to_all | solution.py:128
  138.2 0.4 reshape.141
  138.6 0.2 copy.39
  138.9 5.3 %fusion.31 = (f32[128]{0:T(128)S(1)}, f32[128,3072]{1,0:T(8,128)S(1)}) fusion(bf16[128,1536]{1,0:T(8,128)(2,1)S(1)} %bitcast.94, bf16[1536,3072]{1,0:T(8,128)(2,1)} %param.12), kind=kOutput, calls=%fused_computation.43 | convolution fusion | flops 1208352640 | bytes 11403776 | tf_op jit(solution)/shard_map/dot_general | solution.py:133
  144.2 0.3 multiply_reduce_fusion.1
  144.5 0.7 copy-done.7
  145.2 0.5 convolution_convert_fusion
  145.9 9.3 %all_to_all.51 = bf16[16,2,256]{2,1,0:T(2,128)(2,1)S(1)} all-to-all(bf16[16,2,256]{2,1,0:T(2,128)(2,1)S(1)} %reshape.142), channel_id=1, replica_groups=mesh['groups'=2,'seq'=16] {'seq'}, dimensions={0} | all-to-all | bytes 32768 | tf_op jit(solution)/shard_map/all_to_all | solution.py:143
  155.3 0.2 copy.42
  155.6 0.2 reshape.136
  155.7 0.1 copy.43
  155.9 3.4 %collective-permute-start = (bf16[4,1,64,16]{3,2,1,0:T(8,128)(2,1)S(1)}, bf16[4,1,64,16]{3,2,1,0:T(8,128)(2,1)S(1)}, u32[]{:S(2)}, u32[]{:S(2)}) collective-permute-start(bf16[4,1,64,16]{3,2,1,0:T(8,128)(2,1)S(1)} %get-tuple-element.19), channel_id=1, source_target_pairs={{0,1},{1,2},{2,3},{3,4},{4,5},{5,6},{6,7},{7,8},{8,9},{9,10},{10,1... | collective-permute-start | bytes 24584 | tf_op jit(solution)/shard_map/ppermute | solution.py:24
  159.3 1.9 %collective-permute-start.1 = (bf16[4,1,64,16]{3,2,1,0:T(8,128)(2,1)S(1)}, bf16[4,1,64,16]{3,2,1,0:T(8,128)(2,1)S(1)}, u32[]{:S(2)}, u32[]{:S(2)}) collective-permute-start(bf16[4,1,64,16]{3,2,1,0:T(8,128)(2,1)S(1)} %get-tuple-element.20), channel_id=1, source_target_pairs={{1,0},{2,1},{3,2},{4,3},{5,4},{6,5},{7,6},{8,7},{9,8},{10,9},{11,1... | collective-permute-start | bytes 24584 | tf_op jit(solution)/shard_map/ppermute | solution.py:26
  161.3 4.4 %collective-permute-done.1 = bf16[4,1,64,16]{3,2,1,0:T(8,128)(2,1)S(1)} collective-permute-done((bf16[4,1,64,16]{3,2,1,0:T(8,128)(2,1)S(1)}, bf16[4,1,64,16]{3,2,1,0:T(8,128)(2,1)S(1)}, u32[]{:S(2)}, u32[]{:S(2)}) %collective-permute-start.1) | collective-permute-done | bytes 8224 | tf_op jit(solution)/shard_map/ppermute | solution.py:26
  166.2 0.7 fusion.29
  166.9 0.1 copy.76
  167.1 0.1 pad_maximum_fusion
  167.2 0.2 fusion.27
  167.5 0.1 copy.49
  167.8 0.1 copy.52
  167.9 0.1 copy.53
  168.0 0.1 copy.55
  168.2 0.1 copy.56
  168.3 0.1 copy.58
  168.4 0.1 copy.59
  168.6 0.1 copy.61
  168.7 0.1 copy.62
  168.8 0.1 copy.64
  169.1 0.1 copy.69
  169.2 0.1 copy.70
  169.5 0.1 copy.73
  169.6 0.1 copy.77
  169.9 0.9 copy.51
  170.7 1.5 copy.54
  172.3 0.8 copy.57
  173.0 0.8 copy.60
  173.8 0.8 copy.63
  174.6 3.6 %concatenate.128 = bf16[512,432]{1,0:T(8,128)(2,1)} concatenate(bf16[512,16]{1,0:T(8,128)(2,1)S(1)} %bitcast.102, bf16[512,16]{1,0:T(8,128)(2,1)S(1)} %bitcast.120, bf16[512,16]{1,0:T(8,128)(2,1)S(1)} %bitcast.103, bf16[512,16]{1,0:T(8,128)(2,1)S(1)} %bitcast.104, bf16[512,16]{1,0:T(8,128)(2,1)S(1)} %bitcast.121, bf16[512,16]{1,0:T(8,128)(2,1)S(1)} %bitcast.105, ...), dimensions={1} | concatenate | bytes 884736 | tf_op jit(solution)/shard_map/concatenate | solution.py:94
  178.1 2.3 %fusion.9 = bf16[512,512]{1,0:T(8,128)(2,1)} fusion(bf16[512,432]{1,0:T(8,128)(2,1)} %concatenate.128, bf16[432,512]{1,0:T(8,128)(2,1)S(1)} %copy-done, f32[512]{0:T(512)S(1)} %copy-done.9), kind=kOutput, calls=%fused_computation.11 | convolution fusion | flops 227016704 | bytes 1411072 | tf_op jit(solution)/shard_map/dot_general | solution.py:96
  (50 shorter events, 2.0 us)
Async XLA Ops:
  0.0 178.1 %copy-start = (bf16[432,512]{1,0:T(8,128)(2,1)S(1)}, bf16[432,512]{1,0:T(8,128)(2,1)}, u32[]{:S(2)}) copy-start(bf16[432,512]{1,0:T(8,128)(2,1)} %param.16) | copy-start | bytes 1327108
  0.0 8.6 %copy-start.3 = (bf16[128,1536]{1,0:T(8,128)(2,1)S(1)}, bf16[128,1536]{1,0:T(8,128)(2,1)}, u32[]{:S(2)}) copy-start(bf16[128,1536]{1,0:T(8,128)(2,1)} %param.10) | copy-start | bytes 1179652
  2.0 17.8 %all-to-all-start = ((bf16[16,32,384]{2,1,0:T(8,128)(2,1)}), bf16[16,32,384]{2,1,0:T(8,128)(2,1)S(1)}, u32[]{:S(2)}, u32[]{:S(2)}) async-start(bf16[16,32,384]{2,1,0:T(8,128)(2,1)} %bitcast.1), calls=%async_computation | async-start | bytes 786432 | tf_op jit(solution)/shard_map/all_to_all | solution.py:108
  21.2 4.8 %copy-start.4 = (bf16[128,1536]{1,0:T(8,128)(2,1)S(1)}, bf16[128,1536]{1,0:T(8,128)(2,1)}, u32[]{:S(2)}) copy-start(bf16[128,1536]{1,0:T(8,128)(2,1)} %param.11) | copy-start | bytes 1179652
  21.2 38.2 %all-to-all-start.1 = ((bf16[16,128,384]{1,2,0:T(8,128)(2,1)}), bf16[16,128,384]{1,2,0:T(8,128)(2,1)S(1)}, u32[]{:S(2)}, u32[]{:S(2)}) async-start(bf16[16,128,384]{1,2,0:T(8,128)(2,1)} %bitcast.87), calls=%async_computation.1 | async-start | bytes 3145728 | tf_op jit(solution)/shard_map/all_to_all | solution.py:121
  59.5 1.7 copy-start.2
  61.2 40.9 %all-to-all-start.2 = ((bf16[16,128,384]{1,2,0:T(8,128)(2,1)}), bf16[16,128,384]{1,2,0:T(8,128)(2,1)S(1)}, u32[]{:S(2)}, u32[]{:S(2)}) async-start(bf16[16,128,384]{1,2,0:T(8,128)(2,1)} %bitcast.86), calls=%async_computation.2 | async-start | bytes 3145728 | tf_op jit(solution)/shard_map/all_to_all | solution.py:122
  79.4 4.5 %copy-start.1 = (f32[3,512,2048]{2,1,0:T(8,128)}, f32[3,512,2048]{2,1,0:T(8,128)S(1)}, u32[]{:S(2)}) copy-start(f32[3,512,2048]{2,1,0:T(8,128)S(1)} %get-tuple-element.63) | copy-start | bytes 37748740
  115.1 11.9 %copy-start.6 = (f32[3072]{0:T(1024)S(1)}, f32[3072]{0:T(1024)}, u32[]{:S(2)}) copy-start(f32[3072]{0:T(1024)} %param.14) | copy-start | bytes 36868
  119.5 18.7 %all-to-all-start.3 = ((bf16[16,2,6144]{2,1,0:T(2,128)(2,1)}), bf16[16,2,6144]{2,1,0:T(2,128)(2,1)S(1)}, u32[]{:S(2)}, u32[]{:S(2)}) async-start(bf16[16,2,6144]{2,1,0:T(2,128)(2,1)} %reshape.140), calls=%async_computation.3 | async-start | bytes 786432 | tf_op jit(solution)/shard_map/all_to_all | solution.py:128
  144.2 1.0 copy-start.7
  144.2 1.0 copy-start.8
  155.9 5.4 %collective-permute-start = (bf16[4,1,64,16]{3,2,1,0:T(8,128)(2,1)S(1)}, bf16[4,1,64,16]{3,2,1,0:T(8,128)(2,1)S(1)}, u32[]{:S(2)}, u32[]{:S(2)}) collective-permute-start(bf16[4,1,64,16]{3,2,1,0:T(8,128)(2,1)S(1)} %get-tuple-element.19), channel_id=1, source_target_pairs={{0,1},{1,2},{2,3},{3,4},{4,5},{5,6},{6,7},{7,8},{8,9},{9,10},{10,1... | collective-permute-start | bytes 24584 | tf_op jit(solution)/shard_map/ppermute | solution.py:24
  159.3 6.5 %collective-permute-start.1 = (bf16[4,1,64,16]{3,2,1,0:T(8,128)(2,1)S(1)}, bf16[4,1,64,16]{3,2,1,0:T(8,128)(2,1)S(1)}, u32[]{:S(2)}, u32[]{:S(2)}) collective-permute-start(bf16[4,1,64,16]{3,2,1,0:T(8,128)(2,1)S(1)} %get-tuple-element.20), channel_id=1, source_target_pairs={{1,0},{2,1},{3,2},{4,3},{5,4},{6,5},{7,6},{8,7},{9,8},{10,9},{11,1... | collective-permute-start | bytes 24584 | tf_op jit(solution)/shard_map/ppermute | solution.py:26
  167.6 4.6 %copy-start.5 = (bf16[4,2,64,16]{2,3,1,0:T(8,128)(2,1)S(1)}, bf16[4,2,64,16]{2,3,1,0:T(8,128)(2,1)}, u32[]{:S(2)}) copy-start(bf16[4,2,64,16]{2,3,1,0:T(8,128)(2,1)} %get-tuple-element.49) | copy-start | bytes 49156
  174.6 3.6 %copy-start.9 = (f32[512]{0:T(512)S(1)}, f32[512]{0:T(512)}, u32[]{:S(2)}) copy-start(f32[512]{0:T(512)} %param.17) | copy-start | bytes 6148
where the time goes:
time: 182 us; the launch traced here: 180 us
  waiting for transfers between devices  77.6 us (43%)
  local copies, waits for them, and re-layouts  36.9 us (20%)
  starting transfers between devices  31.7 us (17%)
  matrix products  18.4 us (10%)
  blocking collectives  9.28 us (5%)
  other arithmetic  6.04 us (3%)
    all_to_all x1, waiting for transfers between devices, shards(): lax.all_to_all(key_copies, 'seq', split_axis=0, concat_axis=1, tiled=True)  33.1 us
    all_to_all x1, waiting for transfers between devices, shards(): lax.all_to_all(value_copies, 'seq', split_axis=0, concat_axis=1, tiled=True)  18.2 us
    all_to_all x1, waiting for transfers between devices, shards(): lax.all_to_all(result, 'seq', split_axis=1, concat_axis=0, tiled=True)  11.1 us
    all_to_all x1, waiting for transfers between devices, shards(): lax.all_to_all(to_pieces(queries, blocks), 'seq', split_axis=0, concat_ax...  10.7 us
    all_to_all x1, blocking collectives, shards(): tile = lax.all_to_all(laid, 'seq', split_axis=1, concat_axis=0, tiled=True)  9.28 us
    slice x28, local copies, waits for them, and re-layouts, convolve(): padded[shift_t:shift_t + frames, shift_x:shift_x + width, shift_y:shift_y...  8.1 us
    all_to_all x1, starting transfers between devices, shards(): lax.all_to_all(result, 'seq', split_axis=1, concat_axis=0, tiled=True)  7.52 us
    all_to_all x1, starting transfers between devices, shards(): lax.all_to_all(value_copies, 'seq', split_axis=0, concat_axis=1, tiled=True)  7.5 us
  transfers between devices with their start and end apart: 6, of which 5 were waited for; matrix products, arithmetic and copies ran while one was open for 8% of the time, Pallas kernels for 0%

commit v1 on v0

--- a/solution.py
+++ b/solution.py
@@ -11,6 +11,22 @@
 FRAMES = 4
 ROWS = 32
 COLS_DEV = 1
+
+
+def swapped_with_each(x, axis, split, join):
+    ways, here = (lax.axis_size(axis), lax.axis_index(axis))
+    width = x.shape[split] // ways
+    dims = list(x.shape)
+    dims[split] = width
+    height = dims[join]
+    dims[join] = height * ways
+    full = jnp.zeros(dims, x.dtype)
+    for mask in range(ways):
+        part = lax.dynamic_slice_in_dim(x, (here ^ mask) * width, width, axis=split)
+        if mask:
+            part = lax.ppermute(part, axis, [(d, d ^ mask) for d in range(ways)])
+        full = lax.dynamic_update_slice_in_dim(full, part, (here ^ mask) * height, axis=join)
+    return full
 
 
 def with_halo(cells, sides, width):
@@ -105,9 +121,7 @@
     per_head = HEADS // HEAD_GROUPS
     group_width = per_head * HEAD_DIM
     query_count = tok_dev * HEAD_GROUPS
-    got_queries = lax.all_to_all(
-        to_pieces(queries, blocks), "seq", split_axis=0, concat_axis=1, tiled=True
-    )
+    got_queries = swapped_with_each(to_pieces(queries, blocks), "seq", 0, 1)
     query_rows = got_queries.reshape(query_count, per_head, HEAD_DIM)
     key_groups = jnp.transpose(keys.reshape(tok_dev, HEAD_GROUPS, group_width), (1, 0, 2))
     value_groups = jnp.transpose(values.reshape(tok_dev, HEAD_GROUPS, group_width), (1, 0, 2))

time: 182 us -> 204 us (1.12)
  starting transfers between devices: 31.7 us -> 54 us
  waiting for transfers between devices: 77.6 us -> 65.8 us
  local copies, waits for them, and re-layouts: 36.9 us -> 48.1 us
    ppermute x0 -> x15, starting transfers between devices: none -> 28.2 us  [swapped_with_each(): part = lax.ppermute(part, axis, [(d, d ^ mask) for d in range(ways)])]
    all_to_all x1, waiting for transfers between devices: 18.2 us -> 0.01 us  [shards(): lax.all_to_all(value_copies, 'seq', split_axis=0, concat_axis=1, tiled=True)]
    ppermute x0 -> x15, waiting for transfers between devices: none -> 17.3 us  [swapped_with_each(): part = lax.ppermute(part, axis, [(d, d ^ mask) for d in range(ways)])]
    dynamic_update_slice x0 -> x16, local copies, waits for them, and re-layouts: none -> 10.7 us  [swapped_with_each(): lax.dynamic_update_slice_in_dim(full, part, (here ^ mask) * height, axis=...]
    all_to_all x1 -> x0, waiting for transfers between devices: 10.7 us -> none  [shards(): lax.all_to_all(to_pieces(queries, blocks), 'seq', split_axis=0, concat_ax...]
    all_to_all x1 -> x0, starting transfers between devices: 6.63 us -> none  [shards(): lax.all_to_all(to_pieces(queries, blocks), 'seq', split_axis=0, concat_ax...]
    unnamed x27 -> x29, local copies, waits for them, and re-layouts: 4.76 us -> 4.74 us
  transfers between devices with their start and end apart: 6 -> 20, of which waited for: 5 -> 6; matrix products, arithmetic and copies ran while one was open for 8% -> 13% of each run, Pallas kernels for 0% -> 0%
where the time goes in v1:
time: 204 us; the launch traced here: 203 us
  waiting for transfers between devices  65.8 us (32%)
  starting transfers between devices  54 us (26%)
  local copies, waits for them, and re-layouts  48.1 us (24%)
  matrix products  18.5 us (9%)
  blocking collectives  9.28 us (5%)
  other arithmetic  6.04 us (3%)
    all_to_all x1, waiting for transfers between devices, shards(): lax.all_to_all(key_copies, 'seq', split_axis=0, concat_axis=1, tiled=True)  33 us
    ppermute x15, starting transfers between devices, swapped_with_each(): part = lax.ppermute(part, axis, [(d, d ^ mask) for d in range(ways)])  28.2 us
    ppermute x15, waiting for transfers between devices, swapped_with_each(): part = lax.ppermute(part, axis, [(d, d ^ mask) for d in range(ways)])  17.3 us
    all_to_all x1, waiting for transfers between devices, shards(): lax.all_to_all(result, 'seq', split_axis=1, concat_axis=0, tiled=True)  11.1 us
    dynamic_update_slice x16, local copies, waits for them, and re-layouts, swapped_with_each(): lax.dynamic_update_slice_in_dim(full, part, (here ^ mask) * height, axis=...  10.7 us
    all_to_all x1, blocking collectives, shards(): tile = lax.all_to_all(laid, 'seq', split_axis=1, concat_axis=0, tiled=True)  9.28 us
    all_to_all x1, starting transfers between devices, shards(): lax.all_to_all(value_copies, 'seq', split_axis=0, concat_axis=1, tiled=True)  7.65 us
    slice x28, local copies, waits for them, and re-layouts, convolve(): padded[shift_t:shift_t + frames, shift_x:shift_x + width, shift_y:shift_y...  7.22 us
  transfers between devices with their start and end apart: 20, of which 6 were waited for; matrix products, arithmetic and copies ran while one was open for 13% of the time, Pallas kernels for 0%

profile of v1, /device:TPU:3, one launch (start us, length us, event | category | flops | bytes accessed | tf_op | source)
XLA Modules:
  0.0 202.5 jit_solution(2513541643188219910)
XLA Ops:
  0.0 1.1 reshape.124
  1.5 1.5 broadcast_in_dim.18
  3.0 6.8 %all-to-all-start = ((bf16[16,128,384]{1,2,0:T(8,128)(2,1)}), bf16[16,128,384]{1,2,0:T(8,128)(2,1)S(1)}, u32[]{:S(2)}, u32[]{:S(2)}) async-start(bf16[16,128,384]{1,2,0:T(8,128)(2,1)} %bitcast.89), calls=%async_computation | async-start | bytes 3145728 | tf_op jit(solution)/shard_map/all_to_all | solution.py:135
  10.2 33.0 %all-to-all-done = bf16[16,128,384]{1,2,0:T(8,128)(2,1)S(1)} async-done(((bf16[16,128,384]{1,2,0:T(8,128)(2,1)}), bf16[16,128,384]{1,2,0:T(8,128)(2,1)S(1)}, u32[]{:S(2)}, u32[]{:S(2)}) %all-to-all-start) | async-done | bytes 1572896 | tf_op jit(solution)/shard_map/all_to_all | solution.py:135
  43.2 1.7 broadcast_in_dim.19
  44.9 7.7 %all-to-all-start.1 = ((bf16[16,128,384]{1,2,0:T(8,128)(2,1)}), bf16[16,128,384]{1,2,0:T(8,128)(2,1)S(1)}, u32[]{:S(2)}, u32[]{:S(2)}) async-start(bf16[16,128,384]{1,2,0:T(8,128)(2,1)} %bitcast.88), calls=%async_computation.1 | async-start | bytes 3145728 | tf_op jit(solution)/shard_map/all_to_all | solution.py:136
  52.9 0.5 collective-permute-start
  53.4 1.7 collective-permute-start.2
  55.1 1.2 collective-permute-start.3
  56.3 0.6 collective-permute-start.4
  56.9 1.2 collective-permute-start.5
  58.1 2.4 %collective-permute-done.1 = bf16[1,32,384]{2,1,0:T(8,128)(2,1)S(1)} collective-permute-done((bf16[1,32,384]{2,1,0:T(8,128)(2,1)S(1)}, bf16[1,32,384]{2,1,0:T(8,128)(2,1)S(1)}, u32[]{:S(2)}, u32[]{:S(2)}) %collective-permute-start.1) | collective-permute-done | bytes 24608 | tf_op jit(solution)/shard_map/ppermute | solution.py:27
  60.5 3.3 %collective-permute-start.6 = (bf16[1,32,384]{2,1,0:T(8,128)(2,1)S(1)}, bf16[1,32,384]{2,1,0:T(8,128)(2,1)S(1)}, u32[]{:S(2)}, u32[]{:S(2)}) collective-permute-start(bf16[1,32,384]{2,1,0:T(8,128)(2,1)S(1)} %get-tuple-element.34), channel_id=1, source_target_pairs={{0,7},{1,6},{2,5},{3,4},{4,3},{5,2},{6,1},{7,0},{8,15},{9,14},{10,... | collective-permute-start | bytes 73736 | tf_op jit(solution)/shard_map/ppermute | solution.py:27
  63.8 4.7 %collective-permute-start.7 = (bf16[1,32,384]{2,1,0:T(8,128)(2,1)S(1)}, bf16[1,32,384]{2,1,0:T(8,128)(2,1)S(1)}, u32[]{:S(2)}, u32[]{:S(2)}) collective-permute-start(bf16[1,32,384]{2,1,0:T(8,128)(2,1)S(1)} %get-tuple-element.33), channel_id=1, source_target_pairs={{0,8},{1,9},{2,10},{3,11},{4,12},{5,13},{6,14},{7,15},{8,0},{9,1},... | collective-permute-start | bytes 73736 | tf_op jit(solution)/shard_map/ppermute | solution.py:27
  68.5 10.1 %collective-permute-done.3 = bf16[1,32,384]{2,1,0:T(8,128)(2,1)S(1)} collective-permute-done((bf16[1,32,384]{2,1,0:T(8,128)(2,1)S(1)}, bf16[1,32,384]{2,1,0:T(8,128)(2,1)S(1)}, u32[]{:S(2)}, u32[]{:S(2)}) %collective-permute-start.3) | collective-permute-done | bytes 24608 | tf_op jit(solution)/shard_map/ppermute | solution.py:27
  78.6 5.6 %collective-permute-start.8 = (bf16[1,32,384]{2,1,0:T(8,128)(2,1)S(1)}, bf16[1,32,384]{2,1,0:T(8,128)(2,1)S(1)}, u32[]{:S(2)}, u32[]{:S(2)}) collective-permute-start(bf16[1,32,384]{2,1,0:T(8,128)(2,1)S(1)} %get-tuple-element.32), channel_id=1, source_target_pairs={{0,9},{1,8},{2,11},{3,10},{4,13},{5,12},{6,15},{7,14},{8,1},{9,0},... | collective-permute-start | bytes 73736 | tf_op jit(solution)/shard_map/ppermute | solution.py:27
  84.3 2.3 %collective-permute-start.10 = (bf16[1,32,384]{2,1,0:T(8,128)(2,1)S(1)}, bf16[1,32,384]{2,1,0:T(8,128)(2,1)S(1)}, u32[]{:S(2)}, u32[]{:S(2)}) collective-permute-start(bf16[1,32,384]{2,1,0:T(8,128)(2,1)S(1)} %get-tuple-element.28), channel_id=1, source_target_pairs={{0,11},{1,10},{2,9},{3,8},{4,15},{5,14},{6,13},{7,12},{8,3},{9,2},... | collective-permute-start | bytes 73736 | tf_op jit(solution)/shard_map/ppermute | solution.py:27
  86.6 0.7 collective-permute-start.11
  87.3 4.7 %collective-permute-done.7 = bf16[1,32,384]{2,1,0:T(8,128)(2,1)S(1)} collective-permute-done((bf16[1,32,384]{2,1,0:T(8,128)(2,1)S(1)}, bf16[1,32,384]{2,1,0:T(8,128)(2,1)S(1)}, u32[]{:S(2)}, u32[]{:S(2)}) %collective-permute-start.7) | collective-permute-done | bytes 24608 | tf_op jit(solution)/shard_map/ppermute | solution.py:27
  92.0 3.1 %collective-permute-start.12 = (bf16[1,32,384]{2,1,0:T(8,128)(2,1)S(1)}, bf16[1,32,384]{2,1,0:T(8,128)(2,1)S(1)}, u32[]{:S(2)}, u32[]{:S(2)}) collective-permute-start(bf16[1,32,384]{2,1,0:T(8,128)(2,1)S(1)} %get-tuple-element.19), channel_id=1, source_target_pairs={{0,13},{1,12},{2,15},{3,14},{4,9},{5,8},{6,11},{7,10},{8,5},{9,4},... | collective-permute-start | bytes 73736 | tf_op jit(solution)/shard_map/ppermute | solution.py:27
  95.0 2.1 %collective-permute-start.13 = (bf16[1,32,384]{2,1,0:T(8,128)(2,1)S(1)}, bf16[1,32,384]{2,1,0:T(8,128)(2,1)S(1)}, u32[]{:S(2)}, u32[]{:S(2)}) collective-permute-start(bf16[1,32,384]{2,1,0:T(8,128)(2,1)S(1)} %get-tuple-element.18), channel_id=1, source_target_pairs={{0,14},{1,15},{2,12},{3,13},{4,10},{5,11},{6,8},{7,9},{8,6},{9,7},... | collective-permute-start | bytes 73736 | tf_op jit(solution)/shard_map/ppermute | solution.py:27
  97.2 1.2 collective-permute-start.14
  98.7 0.8 dynamic_update_slice.48
  99.6 0.8 dynamic_update_slice.49
  100.5 0.8 dynamic_update_slice.50
  101.9 0.8 dynamic_update_slice.52
  102.8 0.8 dynamic_update_slice.53
  103.7 0.8 dynamic_update_slice.54
  105.1 0.8 dynamic_update_slice.56
  106.0 0.8 dynamic_update_slice.57
  106.9 0.8 dynamic_update_slice.58
  108.4 0.7 dynamic_update_slice.60
  109.2 0.7 dynamic_update_slice.61
  110.1 0.7 dynamic_update_slice.62
  110.9 0.5 dynamic_update_slice.63
  111.5 3.6 %copy.81 = bf16[16,128,384]{1,0,2:T(8,128)(2,1)} copy(bf16[16,128,384]{1,2,0:T(8,128)(2,1)} %copy-done.2) | data formatting | bytes 3145728 | tf_op jit(solution)/shard_map/all_to_all | solution.py:135
  115.0 3.7 %squeeze.9 = bf16[2048,3,128]{0,2,1:T(8,128)(2,1)} reshape(bf16[16,128,384]{1,0,2:T(8,128)(2,1)} %copy.81) | data formatting | bytes 3145728 | tf_op jit(solution)/shard_map/while/body/jit(dynamic_index_in_dim)/squeeze | solution.py:85
  118.7 3.3 %multiply_reduce_fusion = (f32[3,512]{1,0:T(4,128)S(1)}, f32[3,512,2048]{2,1,0:T(8,128)S(1)}) fusion(bf16[512,3,128]{0,2,1:T(8,128)(2,1)S(1)} %bitcast.103, bf16[2048,3,128]{0,2,1:T(8,128)(2,1)} %squeeze.9), kind=kOutput, calls=%fused_computation.1 | convolution fusion | flops 811596288 | bytes 14555136 | tf_op jit(solution)/shard_map/while/body/eval_jaxpr/qhd,khd->hqk/dot_general | solution.py:69
  122.1 2.5 %fusion = f32[3,512]{1,0:T(4,128)S(1)} fusion(f32[3,512,2048]{2,1,0:T(8,128)S(1)} %get-tuple-element.79, f32[3,512]{1,0:T(4,128)S(1)} %get-tuple-element.77), kind=kLoop, calls=%fused_computation.2 | loop fusion | flops 9435648 | bytes 12595200 | tf_op jit(solution)/shard_map/while/body/eval_jaxpr/reduce_sum | solution.py:75
  124.6 2.0 copy-done.1
  126.6 2.2 %copy.85 = bf16[16,128,384]{1,0,2:T(8,128)(2,1)} copy(bf16[16,128,384]{1,2,0:T(8,128)(2,1)S(1)} %all-to-all-done.1) | data formatting | bytes 3145728 | tf_op jit(solution)/shard_map/all_to_all | solution.py:136
  128.8 2.5 %squeeze.10 = bf16[2048,3,128]{0,2,1:T(8,128)(2,1)S(1)} reshape(bf16[16,128,384]{1,0,2:T(8,128)(2,1)} %copy.85) | data formatting | bytes 3145728 | tf_op jit(solution)/shard_map/while/body/jit(dynamic_index_in_dim)/squeeze | solution.py:85
  131.3 7.1 %fusion.16 = bf16[512,3,128]{0,2,1:T(8,128)(2,1)S(1)} fusion(bf16[2048,3,128]{0,2,1:T(8,128)(2,1)S(1)} %squeeze.10, f32[3,512,2048]{2,1,0:T(8,128)} %copy-done.1, f32[3,512]{1,0:T(4,128)S(1)} %get-tuple-element.77, f32[512,3]{0,1:T(4,128)S(1)} %bitcast_add_fusion, f32[512,3]{0,1:T(4,128)S(1)} %get-tuple-element.76), kind=kOutput, calls=%fused_computation.15 | convolution fusion | flops 815333376 | bytes 14567424 | tf_op jit(solution)/shard_map/while/body/eval_jaxpr/hqk,khd->hqd/dot_general | solution.py:76
  138.5 1.1 copy.86
  139.6 0.5 broadcast.84
  140.1 3.0 %reduce = bf16[512,384]{1,0:T(8,128)(2,1)S(1)} reduce(bf16[512,1,384]{2,1,0:T(2,128)(2,1)S(1)} %bitcast.94, bf16[]{:T(256)} %broadcast.84), dimensions={1}, to_apply=%bitcast.72.reduce_sub_computation | reduce | bytes 786434
  143.1 0.8 reshape.136
  144.0 6.0 %all-to-all-start.2 = ((bf16[16,2,6144]{2,1,0:T(2,128)(2,1)}), bf16[16,2,6144]{2,1,0:T(2,128)(2,1)S(1)}, u32[]{:S(2)}, u32[]{:S(2)}) async-start(bf16[16,2,6144]{2,1,0:T(2,128)(2,1)} %reshape.136), calls=%async_computation.2 | async-start | bytes 786432 | tf_op jit(solution)/shard_map/all_to_all | solution.py:142
  150.0 11.1 %all-to-all-done.2 = bf16[16,2,6144]{2,1,0:T(2,128)(2,1)S(1)} async-done(((bf16[16,2,6144]{2,1,0:T(2,128)(2,1)}), bf16[16,2,6144]{2,1,0:T(2,128)(2,1)S(1)}, u32[]{:S(2)}, u32[]{:S(2)}) %all-to-all-start.2) | async-done | bytes 393248 | tf_op jit(solution)/shard_map/all_to_all | solution.py:142
  161.8 5.3 %fusion.29 = (f32[128]{0:T(128)S(1)}, f32[128,3072]{1,0:T(8,128)S(1)}) fusion(bf16[128,1536]{1,0:T(8,128)(2,1)S(1)} %bitcast.96, bf16[1536,3072]{1,0:T(8,128)(2,1)} %param.12), kind=kOutput, calls=%fused_computation.57 | convolution fusion | flops 1208352640 | bytes 11403776 | tf_op jit(solution)/shard_map/dot_general | solution.py:147
  167.4 0.7 copy-done.8
  168.1 0.5 convolution_convert_fusion
  168.8 9.3 %all_to_all.42 = bf16[16,2,256]{2,1,0:T(2,128)(2,1)S(1)} all-to-all(bf16[16,2,256]{2,1,0:T(2,128)(2,1)S(1)} %reshape.138), channel_id=1, replica_groups=mesh['groups'=2,'seq'=16] {'seq'}, dimensions={0} | all-to-all | bytes 32768 | tf_op jit(solution)/shard_map/all_to_all | solution.py:157
  178.8 3.4 %collective-permute-start.15 = (bf16[4,1,64,16]{3,2,1,0:T(8,128)(2,1)S(1)}, bf16[4,1,64,16]{3,2,1,0:T(8,128)(2,1)S(1)}, u32[]{:S(2)}, u32[]{:S(2)}) collective-permute-start(bf16[4,1,64,16]{3,2,1,0:T(8,128)(2,1)S(1)} %get-tuple-element.44), channel_id=1, source_target_pairs={{0,1},{1,2},{2,3},{3,4},{4,5},{5,6},{6,7},{7,8},{8,9},{9,10},{10,1... | collective-permute-start | bytes 24584 | tf_op jit(solution)/shard_map/ppermute | solution.py:40
  182.2 1.9 collective-permute-start.16
  184.2 4.4 %collective-permute-done.16 = bf16[4,1,64,16]{3,2,1,0:T(8,128)(2,1)S(1)} collective-permute-done((bf16[4,1,64,16]{3,2,1,0:T(8,128)(2,1)S(1)}, bf16[4,1,64,16]{3,2,1,0:T(8,128)(2,1)S(1)}, u32[]{:S(2)}, u32[]{:S(2)}) %collective-permute-start.16) | collective-permute-done | bytes 8224 | tf_op jit(solution)/shard_map/ppermute | solution.py:42
  189.1 0.6 fusion.27
  192.8 0.8 copy.99
  193.6 0.8 copy.102
  194.3 0.8 copy.105
  195.1 0.8 copy.108
  195.8 0.8 copy.111
  196.6 3.6 %concatenate.128 = bf16[512,432]{1,0:T(8,128)(2,1)} concatenate(bf16[512,16]{1,0:T(8,128)(2,1)S(1)} %bitcast.106, bf16[512,16]{1,0:T(8,128)(2,1)S(1)} %bitcast.124, bf16[512,16]{1,0:T(8,128)(2,1)S(1)} %bitcast.107, bf16[512,16]{1,0:T(8,128)(2,1)S(1)} %bitcast.108, bf16[512,16]{1,0:T(8,128)(2,1)} %bitcast.125, bf16[512,16]{1,0:T(8,128)(2,1)S(1)} %bitcast.109, ...), dimensions={1} | concatenate | bytes 884736 | tf_op jit(solution)/shard_map/concatenate | solution.py:110
  200.2 2.3 %fusion.9 = bf16[512,512]{1,0:T(8,128)(2,1)} fusion(bf16[512,432]{1,0:T(8,128)(2,1)} %concatenate.128, bf16[432,512]{1,0:T(8,128)(2,1)S(1)} %copy-done, f32[512]{0:T(512)S(1)} %copy-done.10), kind=kOutput, calls=%fused_computation.11 | convolution fusion | flops 227016704 | bytes 1411072 | tf_op jit(solution)/shard_map/dot_general | solution.py:112
  (113 shorter events, 9.7 us)
Async XLA Ops:
  0.0 200.2 %copy-start = (bf16[432,512]{1,0:T(8,128)(2,1)S(1)}, bf16[432,512]{1,0:T(8,128)(2,1)}, u32[]{:S(2)}) copy-start(bf16[432,512]{1,0:T(8,128)(2,1)} %param.16) | copy-start | bytes 1327108
  3.0 6.8 %copy-start.3 = (bf16[128,1536]{1,0:T(8,128)(2,1)S(1)}, bf16[128,1536]{1,0:T(8,128)(2,1)}, u32[]{:S(2)}) copy-start(bf16[128,1536]{1,0:T(8,128)(2,1)} %param.11) | copy-start | bytes 1179652
  3.0 40.2 %all-to-all-start = ((bf16[16,128,384]{1,2,0:T(8,128)(2,1)}), bf16[16,128,384]{1,2,0:T(8,128)(2,1)S(1)}, u32[]{:S(2)}, u32[]{:S(2)}) async-start(bf16[16,128,384]{1,2,0:T(8,128)(2,1)} %bitcast.89), calls=%async_computation | async-start | bytes 3145728 | tf_op jit(solution)/shard_map/all_to_all | solution.py:135
  43.2 1.7 copy-start.2
  44.9 7.7 %copy-start.4 = (bf16[128,1536]{1,0:T(8,128)(2,1)S(1)}, bf16[128,1536]{1,0:T(8,128)(2,1)}, u32[]{:S(2)}) copy-start(bf16[128,1536]{1,0:T(8,128)(2,1)} %param.9) | copy-start | bytes 1179652
  44.9 81.7 %all-to-all-start.1 = ((bf16[16,128,384]{1,2,0:T(8,128)(2,1)}), bf16[16,128,384]{1,2,0:T(8,128)(2,1)S(1)}, u32[]{:S(2)}, u32[]{:S(2)}) async-start(bf16[16,128,384]{1,2,0:T(8,128)(2,1)} %bitcast.88), calls=%async_computation.1 | async-start | bytes 3145728 | tf_op jit(solution)/shard_map/all_to_all | solution.py:136
  52.9 4.0 %collective-permute-start = (bf16[1,32,384]{2,1,0:T(8,128)(2,1)S(1)}, bf16[1,32,384]{2,1,0:T(8,128)(2,1)S(1)}, u32[]{:S(2)}, u32[]{:S(2)}) collective-permute-start(bf16[1,32,384]{2,1,0:T(8,128)(2,1)S(1)} %get-tuple-element.40), channel_id=1, source_target_pairs={{0,1},{1,0},{2,3},{3,2},{4,5},{5,4},{6,7},{7,6},{8,9},{9,8},{10,11... | collective-permute-start | bytes 73736 | tf_op jit(solution)/shard_map/ppermute | solution.py:27
  53.4 7.1 %collective-permute-start.1 = (bf16[1,32,384]{2,1,0:T(8,128)(2,1)S(1)}, bf16[1,32,384]{2,1,0:T(8,128)(2,1)S(1)}, u32[]{:S(2)}, u32[]{:S(2)}) collective-permute-start(bf16[1,32,384]{2,1,0:T(8,128)(2,1)S(1)} %get-tuple-element.39), channel_id=1, source_target_pairs={{0,2},{1,3},{2,0},{3,1},{4,6},{5,7},{6,4},{7,5},{8,10},{9,11},{10,... | collective-permute-start | bytes 73736 | tf_op jit(solution)/shard_map/ppermute | solution.py:27
  53.4 10.4 %collective-permute-start.2 = (bf16[1,32,384]{2,1,0:T(8,128)(2,1)S(1)}, bf16[1,32,384]{2,1,0:T(8,128)(2,1)S(1)}, u32[]{:S(2)}, u32[]{:S(2)}) collective-permute-start(bf16[1,32,384]{2,1,0:T(8,128)(2,1)S(1)} %get-tuple-element.38), channel_id=1, source_target_pairs={{0,3},{1,2},{2,1},{3,0},{4,7},{5,6},{6,5},{7,4},{8,11},{9,10},{10,... | collective-permute-start | bytes 73736 | tf_op jit(solution)/shard_map/ppermute | solution.py:27
  55.1 23.5 %collective-permute-start.3 = (bf16[1,32,384]{2,1,0:T(8,128)(2,1)S(1)}, bf16[1,32,384]{2,1,0:T(8,128)(2,1)S(1)}, u32[]{:S(2)}, u32[]{:S(2)}) collective-permute-start(bf16[1,32,384]{2,1,0:T(8,128)(2,1)S(1)} %get-tuple-element.37), channel_id=1, source_target_pairs={{0,4},{1,5},{2,6},{3,7},{4,0},{5,1},{6,2},{7,3},{8,12},{9,13},{10,... | collective-permute-start | bytes 73736 | tf_op jit(solution)/shard_map/ppermute | solution.py:27
  56.3 27.9 %collective-permute-start.4 = (bf16[1,32,384]{2,1,0:T(8,128)(2,1)S(1)}, bf16[1,32,384]{2,1,0:T(8,128)(2,1)S(1)}, u32[]{:S(2)}, u32[]{:S(2)}) collective-permute-start(bf16[1,32,384]{2,1,0:T(8,128)(2,1)S(1)} %get-tuple-element.36), channel_id=1, source_target_pairs={{0,5},{1,4},{2,7},{3,6},{4,1},{5,0},{6,3},{7,2},{8,13},{9,12},{10,... | collective-permute-start | bytes 73736 | tf_op jit(solution)/shard_map/ppermute | solution.py:27
  56.9 27.5 %collective-permute-start.5 = (bf16[1,32,384]{2,1,0:T(8,128)(2,1)S(1)}, bf16[1,32,384]{2,1,0:T(8,128)(2,1)S(1)}, u32[]{:S(2)}, u32[]{:S(2)}) collective-permute-start(bf16[1,32,384]{2,1,0:T(8,128)(2,1)S(1)} %get-tuple-element.35), channel_id=1, source_target_pairs={{0,6},{1,7},{2,4},{3,5},{4,2},{5,3},{6,0},{7,1},{8,14},{9,15},{10,... | collective-permute-start | bytes 73736 | tf_op jit(solution)/shard_map/ppermute | solution.py:27
  60.5 26.2 %collective-permute-start.6 = (bf16[1,32,384]{2,1,0:T(8,128)(2,1)S(1)}, bf16[1,32,384]{2,1,0:T(8,128)(2,1)S(1)}, u32[]{:S(2)}, u32[]{:S(2)}) collective-permute-start(bf16[1,32,384]{2,1,0:T(8,128)(2,1)S(1)} %get-tuple-element.34), channel_id=1, source_target_pairs={{0,7},{1,6},{2,5},{3,4},{4,3},{5,2},{6,1},{7,0},{8,15},{9,14},{10,... | collective-permute-start | bytes 73736 | tf_op jit(solution)/shard_map/ppermute | solution.py:27
  63.8 28.2 %collective-permute-start.7 = (bf16[1,32,384]{2,1,0:T(8,128)(2,1)S(1)}, bf16[1,32,384]{2,1,0:T(8,128)(2,1)S(1)}, u32[]{:S(2)}, u32[]{:S(2)}) collective-permute-start(bf16[1,32,384]{2,1,0:T(8,128)(2,1)S(1)} %get-tuple-element.33), channel_id=1, source_target_pairs={{0,8},{1,9},{2,10},{3,11},{4,12},{5,13},{6,14},{7,15},{8,0},{9,1},... | collective-permute-start | bytes 73736 | tf_op jit(solution)/shard_map/ppermute | solution.py:27
  78.6 16.4 %collective-permute-start.8 = (bf16[1,32,384]{2,1,0:T(8,128)(2,1)S(1)}, bf16[1,32,384]{2,1,0:T(8,128)(2,1)S(1)}, u32[]{:S(2)}, u32[]{:S(2)}) collective-permute-start(bf16[1,32,384]{2,1,0:T(8,128)(2,1)S(1)} %get-tuple-element.32), channel_id=1, source_target_pairs={{0,9},{1,8},{2,11},{3,10},{4,13},{5,12},{6,15},{7,14},{8,1},{9,0},... | collective-permute-start | bytes 73736 | tf_op jit(solution)/shard_map/ppermute | solution.py:27
  84.2 13.0 %collective-permute-start.9 = (bf16[1,32,384]{2,1,0:T(8,128)(2,1)S(1)}, bf16[1,32,384]{2,1,0:T(8,128)(2,1)S(1)}, u32[]{:S(2)}, u32[]{:S(2)}) collective-permute-start(bf16[1,32,384]{2,1,0:T(8,128)(2,1)S(1)} %get-tuple-element.30), channel_id=1, source_target_pairs={{0,10},{1,11},{2,8},{3,9},{4,14},{5,15},{6,12},{7,13},{8,2},{9,3},... | collective-permute-start | bytes 73736 | tf_op jit(solution)/shard_map/ppermute | solution.py:27
  84.3 23.4 %collective-permute-start.10 = (bf16[1,32,384]{2,1,0:T(8,128)(2,1)S(1)}, bf16[1,32,384]{2,1,0:T(8,128)(2,1)S(1)}, u32[]{:S(2)}, u32[]{:S(2)}) collective-permute-start(bf16[1,32,384]{2,1,0:T(8,128)(2,1)S(1)} %get-tuple-element.28), channel_id=1, source_target_pairs={{0,11},{1,10},{2,9},{3,8},{4,15},{5,14},{6,13},{7,12},{8,3},{9,2},... | collective-permute-start | bytes 73736 | tf_op jit(solution)/shard_map/ppermute | solution.py:27
  86.6 21.7 %collective-permute-start.11 = (bf16[1,32,384]{2,1,0:T(8,128)(2,1)S(1)}, bf16[1,32,384]{2,1,0:T(8,128)(2,1)S(1)}, u32[]{:S(2)}, u32[]{:S(2)}) collective-permute-start(bf16[1,32,384]{2,1,0:T(8,128)(2,1)S(1)} %get-tuple-element.20), channel_id=1, source_target_pairs={{0,12},{1,13},{2,14},{3,15},{4,8},{5,9},{6,10},{7,11},{8,4},{9,5},... | collective-permute-start | bytes 73736 | tf_op jit(solution)/shard_map/ppermute | solution.py:27
  92.0 17.1 %collective-permute-start.12 = (bf16[1,32,384]{2,1,0:T(8,128)(2,1)S(1)}, bf16[1,32,384]{2,1,0:T(8,128)(2,1)S(1)}, u32[]{:S(2)}, u32[]{:S(2)}) collective-permute-start(bf16[1,32,384]{2,1,0:T(8,128)(2,1)S(1)} %get-tuple-element.19), channel_id=1, source_target_pairs={{0,13},{1,12},{2,15},{3,14},{4,9},{5,8},{6,11},{7,10},{8,5},{9,4},... | collective-permute-start | bytes 73736 | tf_op jit(solution)/shard_map/ppermute | solution.py:27
  95.0 14.9 %collective-permute-start.13 = (bf16[1,32,384]{2,1,0:T(8,128)(2,1)S(1)}, bf16[1,32,384]{2,1,0:T(8,128)(2,1)S(1)}, u32[]{:S(2)}, u32[]{:S(2)}) collective-permute-start(bf16[1,32,384]{2,1,0:T(8,128)(2,1)S(1)} %get-tuple-element.18), channel_id=1, source_target_pairs={{0,14},{1,15},{2,12},{3,13},{4,10},{5,11},{6,8},{7,9},{8,6},{9,7},... | collective-permute-start | bytes 73736 | tf_op jit(solution)/shard_map/ppermute | solution.py:27
  97.2 13.6 %collective-permute-start.14 = (bf16[1,32,384]{2,1,0:T(8,128)(2,1)S(1)}, bf16[1,32,384]{2,1,0:T(8,128)(2,1)S(1)}, u32[]{:S(2)}, u32[]{:S(2)}) collective-permute-start(bf16[1,32,384]{2,1,0:T(8,128)(2,1)S(1)} %get-tuple-element.17), channel_id=1, source_target_pairs={{0,15},{1,14},{2,13},{3,12},{4,11},{5,10},{6,9},{7,8},{8,7},{9,6},... | collective-permute-start | bytes 73736 | tf_op jit(solution)/shard_map/ppermute | solution.py:27
  122.1 4.5 %copy-start.1 = (f32[3,512,2048]{2,1,0:T(8,128)}, f32[3,512,2048]{2,1,0:T(8,128)S(1)}, u32[]{:S(2)}) copy-start(f32[3,512,2048]{2,1,0:T(8,128)S(1)} %get-tuple-element.79) | copy-start | bytes 37748740
  139.6 10.4 %copy-start.7 = (f32[3072]{0:T(1024)S(1)}, f32[3072]{0:T(1024)}, u32[]{:S(2)}) copy-start(f32[3072]{0:T(1024)} %param.14) | copy-start | bytes 36868
  144.0 17.2 %all-to-all-start.2 = ((bf16[16,2,6144]{2,1,0:T(2,128)(2,1)}), bf16[16,2,6144]{2,1,0:T(2,128)(2,1)S(1)}, u32[]{:S(2)}, u32[]{:S(2)}) async-start(bf16[16,2,6144]{2,1,0:T(2,128)(2,1)} %reshape.136), calls=%async_computation.2 | async-start | bytes 786432 | tf_op jit(solution)/shard_map/all_to_all | solution.py:142
  167.1 1.0 copy-start.8
  167.1 1.0 copy-start.9
  178.8 5.4 %collective-permute-start.15 = (bf16[4,1,64,16]{3,2,1,0:T(8,128)(2,1)S(1)}, bf16[4,1,64,16]{3,2,1,0:T(8,128)(2,1)S(1)}, u32[]{:S(2)}, u32[]{:S(2)}) collective-permute-start(bf16[4,1,64,16]{3,2,1,0:T(8,128)(2,1)S(1)} %get-tuple-element.44), channel_id=1, source_target_pairs={{0,1},{1,2},{2,3},{3,4},{4,5},{5,6},{6,7},{7,8},{8,9},{9,10},{10,1... | collective-permute-start | bytes 24584 | tf_op jit(solution)/shard_map/ppermute | solution.py:40
  182.2 6.5 %collective-permute-start.16 = (bf16[4,1,64,16]{3,2,1,0:T(8,128)(2,1)S(1)}, bf16[4,1,64,16]{3,2,1,0:T(8,128)(2,1)S(1)}, u32[]{:S(2)}, u32[]{:S(2)}) collective-permute-start(bf16[4,1,64,16]{3,2,1,0:T(8,128)(2,1)S(1)} %get-tuple-element.45), channel_id=1, source_target_pairs={{1,0},{2,1},{3,2},{4,3},{5,4},{6,5},{7,6},{8,7},{9,8},{10,9},{11,1... | collective-permute-start | bytes 24584 | tf_op jit(solution)/shard_map/ppermute | solution.py:42
  190.3 2.4 %copy-start.6 = (bf16[4,2,64,16]{2,3,1,0:T(8,128)(2,1)S(1)}, bf16[4,2,64,16]{2,3,1,0:T(8,128)(2,1)}, u32[]{:S(2)}) copy-start(bf16[4,2,64,16]{2,3,1,0:T(8,128)(2,1)} %get-tuple-element.68) | copy-start | bytes 49156
  190.3 2.5 %copy-start.5 = (bf16[4,2,64,16]{2,3,1,0:T(8,128)(2,1)S(1)}, bf16[4,2,64,16]{2,3,1,0:T(8,128)(2,1)}, u32[]{:S(2)}) copy-start(bf16[4,2,64,16]{2,3,1,0:T(8,128)(2,1)} %get-tuple-element.67) | copy-start | bytes 49156
  196.6 3.6 %copy-start.10 = (f32[512]{0:T(512)S(1)}, f32[512]{0:T(512)}, u32[]{:S(2)}) copy-start(f32[512]{0:T(512)} %param.17) | copy-start | bytes 6148
